TPU v7x, 256 devices: a whole 4x4x8 slice. The times are simulated.
256 devices in a mesh: shot: 32 (over y, x, core), freq: 8 (over z).
Axes of the slice: x: 4, y: 4, z: 8, core: 2. Of those that a mesh axis runs over, the one named last changes fastest.
Arguments:
- traces: float32 [128, 2048, 1024], P('shot', 'freq'), may hold values from -6 to 6
- interp_weights: float32 [128, 16, 128, 128], P('shot'), may hold values from -0.09375 to 0.09375
- tile_ids: int32 [128, 16], P('shot'), may hold values from 0 to 63, as said below
Outputs:
- binned: float32 [64, 2, 384, 128], P('shot', None, 'freq')
Inputs may be any that keep to these rules, and one draw needn't show every extreme that they name: `tile_ids`: tile g is owned by index g // 2 of shot. Among the receiver blocks of the shots of one index of shot, at most 4 land on tiles of one owner, and in every draw each index of shot sends exactly 4 to one owner.
All inputs are finite; a program needn't handle non-finite values.
Results may differ from a plain program's by a relative error of at most 0.0003.
Values sent between devices are 32-bit elements; how exact they have to be, the bound alone decides.
A program may use at most 64 MiB of HBM per device.

v0:
```python
import math

import jax
import jax.numpy as jnp
from jax import lax
from jax.sharding import PartitionSpec as P

NF = 384
TILES_DEV = 2


def shards(traces, interp_weights, tile_ids):
    highest = lax.Precision.HIGHEST
    shot_count = lax.axis_size("shot")
    freq_count = lax.axis_size("freq")
    shots_here = traces.shape[0]
    time_len = traces.shape[2]
    block_count = interp_weights.shape[1]
    block_len = interp_weights.shape[2]
    tile_len = interp_weights.shape[3]
    freq_here = NF // freq_count
    freq_index = jnp.arange(NF, dtype=jnp.int32)
    time_index = jnp.arange(time_len, dtype=jnp.int32)
    phase = freq_index[:, None] * time_index[None, :] % time_len
    angle = phase.astype(jnp.float32) * (2.0 * math.pi / time_len)
    tables = jnp.stack([jnp.cos(angle), -jnp.sin(angle)]) * (1.0 / math.sqrt(time_len))
    spectrum = jnp.einsum("cft,srt->scfr", tables, traces, precision=highest)
    gathered = lax.all_to_all(spectrum, "freq", split_axis=2, concat_axis=3, tiled=True)
    blocks = gathered.reshape(shots_here, 2 * freq_here, block_count, block_len)
    partial_value = jnp.einsum("scbr,sbrt->sbct", blocks, interp_weights, precision=highest)
    row_count = shots_here * block_count
    width = 2 * freq_here * tile_len
    partial_value = partial_value.reshape(row_count, width)
    tile_rows = tile_ids.reshape(row_count)
    cap_slots = (row_count + shot_count - 1) // shot_count + 2
    owner_of = tile_rows // TILES_DEV
    local_tile = tile_rows % TILES_DEV
    owner_hits = (owner_of[:, None] == jnp.arange(shot_count, dtype=jnp.int32)[None, :]).astype(
        jnp.int32
    )
    running = jnp.cumsum(owner_hits, axis=0)
    position = jnp.sum(running * owner_hits, axis=1) - 1
    slot_index = owner_of * cap_slots + position
    slot_range = jnp.arange(shot_count * cap_slots, dtype=jnp.int32)
    placing = slot_index[None, :] == slot_range[:, None]
    send_rows = jnp.dot(placing.astype(jnp.float32), partial_value, precision=highest)
    send_tiles = jnp.sum(jnp.where(placing, local_tile[None, :] + 1, 0), axis=1) - 1
    received, got_tiles = (
        lax.all_to_all(
            send_rows.reshape(shot_count, cap_slots, width),
            "shot",
            split_axis=0,
            concat_axis=0,
            tiled=True,
        ),
        lax.all_to_all(
            send_tiles.reshape(shot_count, cap_slots),
            "shot",
            split_axis=0,
            concat_axis=0,
            tiled=True,
        ),
    )
    landing = (
        got_tiles.reshape(shot_count * cap_slots)[None, :]
        == jnp.arange(TILES_DEV, dtype=jnp.int32)[:, None]
    ).astype(jnp.float32)
    binned = jnp.dot(landing, received.reshape(shot_count * cap_slots, width), precision=highest)
    return binned.reshape(TILES_DEV, 2, freq_here, tile_len)


def solution(mesh):
    in_specs = (P("shot", "freq", None), P("shot", None, None, None), P("shot", None))
    out_specs = P("shot", None, "freq", None)
    return jax.shard_map(shards, mesh=mesh, in_specs=in_specs, out_specs=out_specs, check_vma=False)
```

profile of v0, /device:TPU:1, one launch (start us, length us, event | category | flops | bytes accessed | tf_op | source)
XLA Modules:
  0.0 240.6 jit_solution(3196099352758966526)
XLA Ops:
  0.0 6.2 %sine_negate_fusion = (f32[1,384,1024]{2,1,0:T(8,128)S(1)}, f32[1,384,1024]{2,1,0:T(8,128)S(1)}) fusion(), kind=kLoop, calls=%fused_computation.17 | loop fusion | flops 5898240 | bytes 3145728 | tf_op jit(solution)/shard_map/neg | solution.py:26
  6.2 12.1 %fusion.8 = f32[4,2,384,256]{3,2,0,1:T(8,128)S(1)} fusion(f32[4,256,1024]{2,1,0:T(8,128)} %param.3, f32[1,384,1024]{2,1,0:T(8,128)S(1)} %get-tuple-element.7, f32[1,384,1024]{2,1,0:T(8,128)S(1)} %get-tuple-element.8), kind=kOutput, calls=%fused_computation.12 | convolution fusion | flops 9665249280 | bytes 10485760 | tf_op jit(solution)/shard_map/cft,srt->scfr/dot_general | solution.py:27
  18.3 3.7 %copy.18 = f32[4,2,384,256]{3,0,1,2:T(4,128)} copy(f32[4,2,384,256]{3,2,0,1:T(8,128)S(1)} %fusion.8) | data formatting | bytes 6291456 | tf_op jit(solution)/shard_map/cft,srt->scfr/transpose | solution.py:27
  22.0 9.1 %all-to-all-start.1 = ((f32[4,2,384,256]{3,0,1,2:T(4,128)}), f32[4,2,384,256]{3,0,1,2:T(4,128)S(1)}, u32[]{:S(2)}, u32[]{:S(2)}) async-start(f32[4,2,384,256]{3,0,1,2:T(4,128)} %copy.18), calls=%async_computation.1 | async-start | bytes 6291456 | tf_op jit(solution)/shard_map/all_to_all | solution.py:28
  31.4 0.2 select_reduce_fusion.1
  31.6 0.1 select_reduce_fusion
  31.7 0.7 sub.19
  32.4 72.9 %all-to-all-done.1 = f32[4,2,384,256]{3,0,1,2:T(4,128)S(1)} async-done(((f32[4,2,384,256]{3,0,1,2:T(4,128)}), f32[4,2,384,256]{3,0,1,2:T(4,128)S(1)}, u32[]{:S(2)}, u32[]{:S(2)}) %all-to-all-start.1) | async-done | bytes 3145760 | tf_op jit(solution)/shard_map/all_to_all | solution.py:28
  105.4 7.6 %all-to-all-start = ((s32[32,1,4]{2,1,0:T(1,128)}), s32[32,1,4]{2,1,0:T(1,128)S(1)}, u32[]{:S(2)}, u32[]{:S(2)}) async-start(s32[32,1,4]{2,1,0:T(1,128)} %bitcast), calls=%async_computation | async-start | bytes 32768 | tf_op jit(solution)/shard_map/all_to_all | solution.py:56
  113.0 3.5 %copy.29 = f32[4,2,8,48,256]{4,2,3,1,0:T(8,128)} copy(f32[4,2,8,48,256]{4,0,1,3,2:T(4,128)S(1)} %bitcast.35) | data formatting | bytes 6291456 | tf_op jit(solution)/shard_map/all_to_all | solution.py:28
  116.5 2.7 %reshape.208 = f32[4,96,16,128]{3,2,1,0:T(8,128)S(1)} reshape(f32[4,2,48,8,256]{4,3,2,1,0:T(8,128)} %bitcast.36) | data formatting | bytes 6291456 | tf_op jit(solution)/shard_map/reshape | solution.py:29
  119.2 7.3 %fusion.6 = f32[4,16,96,128]{3,2,1,0:T(8,128)} fusion(f32[4,16,128,128]{3,2,1,0:T(8,128)} %param.4, f32[4,96,16,128]{3,2,1,0:T(8,128)S(1)} %reshape.208), kind=kOutput, calls=%fused_computation.6 | convolution fusion | flops 1207959552 | bytes 10485760 | tf_op jit(solution)/shard_map/scbr,sbrt->sbct/dot_general | solution.py:30
  126.4 2.8 %reshape.213 = f32[64,12288,1]{1,0,2:T(8,128)S(1)} reshape(f32[4,16,96,128]{3,2,1,0:T(8,128)} %fusion.6) | data formatting | bytes 6291456 | tf_op jit(solution)/shard_map/reshape | solution.py:33
  129.3 2.7 %fusion.21 = f32[32,4,12288]{2,0,1:T(8,128)S(1)} fusion(f32[64,12288,1]{1,0,2:T(8,128)S(1)} %reshape.213, s32[32,4]{0,1:T(4,128)S(1)} %multiply_add_fusion, s32[64]{0:T(128)S(1)} %add_add_fusion), kind=kOutput, calls=%fused_computation.22 | convolution fusion | flops 1207967744 | bytes 9437952 | tf_op jit(solution)/shard_map/dot_general | solution.py:46
  132.0 6.7 %copy.21 = f32[32,4,12288]{2,1,0:T(4,128)} copy(f32[32,4,12288]{2,0,1:T(8,128)S(1)} %fusion.21) | data formatting | bytes 12582912 | tf_op jit(solution)/shard_map/dot_general | solution.py:46
  138.7 7.4 %all-to-all-start.2 = ((f32[32,4,12288]{2,1,0:T(4,128)}), f32[32,4,12288]{2,1,0:T(4,128)}, u32[]{:S(2)}, u32[]{:S(2)}) async-start(f32[32,4,12288]{2,1,0:T(4,128)} %copy.21), calls=%async_computation.2 | async-start | bytes 12582912 | tf_op jit(solution)/shard_map/all_to_all | solution.py:49
  146.2 0.5 broadcast.239
  146.7 0.7 reduce.3
  147.4 0.1 eq.68
  147.5 72.3 %all-to-all-done.2 = f32[32,4,12288]{2,1,0:T(4,128)} async-done(((f32[32,4,12288]{2,1,0:T(4,128)}), f32[32,4,12288]{2,1,0:T(4,128)}, u32[]{:S(2)}, u32[]{:S(2)}) %all-to-all-start.2) | async-done | bytes 6291488 | tf_op jit(solution)/shard_map/all_to_all | solution.py:49
  219.8 7.9 %reshape.210 = f32[128,12288]{1,0:T(8,128)} reshape(f32[32,4,12288]{2,1,0:T(4,128)} %all-to-all-done.2) | data formatting | bytes 12582912 | tf_op jit(solution)/shard_map/reshape | solution.py:68
  227.7 6.6 %copy.22 = f32[12288,128]{1,0:T(8,128)} copy(f32[12288,128]{0,1:T(8,128)} %bitcast.34) | data formatting | bytes 12582912 | tf_op jit(solution)/shard_map/dot_general | solution.py:68
  234.3 5.6 %fusion.26 = f32[2,2,48,128]{3,0,2,1:T(2,128)S(1)} fusion(f32[2,48,128,128]{3,2,1,0:T(8,128)} %bitcast.33, s32[128]{0:T(128)S(1)} %eq.68), kind=kOutput, calls=%fused_computation.32 | convolution fusion | flops 37748992 | bytes 6390272 | tf_op jit(solution)/shard_map/dot_general | solution.py:68
  239.9 0.7 copy.23
  (10 shorter events, 0.3 us)
Async XLA Ops:
  22.0 9.1 %copy-start = (s32[4,16]{1,0:T(4,128)S(1)}, s32[4,16]{1,0:T(4,128)}, u32[]{:S(2)}) copy-start(s32[4,16]{1,0:T(4,128)} %param.5) | copy-start | bytes 772
  22.0 83.4 %all-to-all-start.1 = ((f32[4,2,384,256]{3,0,1,2:T(4,128)}), f32[4,2,384,256]{3,0,1,2:T(4,128)S(1)}, u32[]{:S(2)}, u32[]{:S(2)}) async-start(f32[4,2,384,256]{3,0,1,2:T(4,128)} %copy.18), calls=%async_computation.1 | async-start | bytes 6291456 | tf_op jit(solution)/shard_map/all_to_all | solution.py:28
  105.4 33.3 %all-to-all-start = ((s32[32,1,4]{2,1,0:T(1,128)}), s32[32,1,4]{2,1,0:T(1,128)S(1)}, u32[]{:S(2)}, u32[]{:S(2)}) async-start(s32[32,1,4]{2,1,0:T(1,128)} %bitcast), calls=%async_computation | async-start | bytes 32768 | tf_op jit(solution)/shard_map/all_to_all | solution.py:56
  138.7 81.1 %all-to-all-start.2 = ((f32[32,4,12288]{2,1,0:T(4,128)}), f32[32,4,12288]{2,1,0:T(4,128)}, u32[]{:S(2)}, u32[]{:S(2)}) async-start(f32[32,4,12288]{2,1,0:T(4,128)} %copy.21), calls=%async_computation.2 | async-start | bytes 12582912 | tf_op jit(solution)/shard_map/all_to_all | solution.py:49
where the time goes:
time: 243 us; the launch traced here: 241 us
  waiting for transfers between devices  145 us (60%)
  local copies, waits for them, and re-layouts  36 us (15%)
  matrix products  27.8 us (11%)
  starting transfers between devices  24.1 us (10%)
  other arithmetic  7.34 us (3%)
    all_to_all x1, waiting for transfers between devices, shards(): lax.all_to_all(spectrum, 'freq', split_axis=2, concat_axis=3, tiled=True)  72.9 us
    all_to_all x1, waiting for transfers between devices, shards(): lax.all_to_all(send_rows.reshape(shot_count, cap_slots, width), 'shot', s...  72.3 us
    dot_general x1, matrix products, shards(): spectrum = jnp.einsum('cft,srt->scfr', tables, traces, precision=highest)  12.1 us
    all_to_all x1, starting transfers between devices, shards(): lax.all_to_all(spectrum, 'freq', split_axis=2, concat_axis=3, tiled=True)  9.13 us
    reshape x1, local copies, waits for them, and re-layouts, shards(): received.reshape(shot_count * cap_slots, width)  7.92 us
    all_to_all x1, starting transfers between devices, shards(): lax.all_to_all(send_tiles.reshape(shot_count, cap_slots), 'shot', split_a...  7.59 us
    all_to_all x1, starting transfers between devices, shards(): lax.all_to_all(send_rows.reshape(shot_count, cap_slots, width), 'shot', s...  7.43 us
    dot_general x1, matrix products, shards(): jnp.einsum('scbr,sbrt->sbct', blocks, interp_weights, precision=highest)  7.28 us
  transfers between devices with their start and end apart: 3, of which 2 were waited for; matrix products, arithmetic and copies ran while one was open for 12% of the time, Pallas kernels for 0%

commit v1 on v0

v1 whole, which is shorter than its diff:
```python
import math

import jax
import jax.numpy as jnp
import numpy as np
from jax import lax
from jax.experimental import pallas as pl
from jax.experimental.pallas import tpu as pltpu
from jax.sharding import PartitionSpec as P

NF = 384
TILES_DEV = 2
YS, XS, CS = 4, 4, 2
PLANE = YS * XS * CS
ZS = 8
ROWS = 8
MESH = pl.DeviceIdType.MESH


def tables(time_len, per):
    t = np.arange(time_len)
    low = 2.0 * math.pi / time_len * (np.arange(per)[:, None] * t[None, :] % time_len)
    base = np.concatenate([np.cos(low), np.sin(low)]) / math.sqrt(time_len)
    high = 2.0 * math.pi / time_len * ((np.arange(ZS) * per)[:, None] * t[None, :] % time_len)
    turn = np.stack([np.cos(high), np.sin(high)], axis=1)
    return base.astype(np.float32), turn.astype(np.float32)


def split(value):
    high = value.astype(jnp.bfloat16)
    return high, (value - high.astype(jnp.float32)).astype(jnp.bfloat16)


def nt_dot(a, b):
    return lax.dot_general(a, b, (((1,), (1,)), ((), ())), preferred_element_type=jnp.float32)


def nn_dot(a, b):
    return jnp.dot(a, b, preferred_element_type=jnp.float32)


def kernel(
    ids_ref, base_ref, turn_ref, traces_ref, weights_ref, out_ref,
    tr, tr_hi, tr_lo, wt, wt_hi, wt_lo, table, send, recv, zsend, zrecv,
    id_send, id_recv, onehot, fsend, frecv,
    load_sem, wload_sem, send_sem, recv_sem, self_sem, zsend_sem, zrecv_sem,
    id_send_sem, id_recv_sem, fsend_sem, frecv_sem, fself_sem,
):
    per = base_ref.shape[0] // 2
    both = 2 * per
    share = both // PLANE
    tiles = PLANE * TILES_DEV
    me = lax.axis_index("shot")
    z = lax.axis_index("freq")
    core = me % CS
    x = me // CS % XS
    y = me // (CS * XS)

    def peer(r):
        py = (y + r // (CS * XS)) % YS
        px = (x + r // CS % XS) % XS
        pc = (core + r) % CS
        return (py * XS + px) * CS + pc

    barrier = pltpu.get_barrier_semaphore()

    def greet(r, carry):
        pl.semaphore_signal(barrier, inc=1, device_id=(peer(r), z), device_id_type=MESH)
        return carry

    lax.fori_loop(1, PLANE, greet, 0)
    for step in (1, ZS - 1):
        pl.semaphore_signal(
            barrier, inc=1, device_id=(me, (z + step) % ZS), device_id_type=MESH
        )

    shots = traces_ref.shape[0]
    per_shot = traces_ref.shape[1]
    loads = []
    for s in range(shots):
        loads.append(
            pltpu.make_async_copy(
                traces_ref.at[s], tr.at[pl.ds(s * per_shot, per_shot)], load_sem.at[s]
            )
        )
        loads[-1].start()
    wloads = []
    for s in range(shots):
        wloads.append(
            pltpu.make_async_copy(
                weights_ref.at[s, pl.ds(2 * z, 2)], wt.at[pl.ds(2 * s, 2)], wload_sem.at[s]
            )
        )
        wloads[-1].start()

    sub = lax.broadcasted_iota(jnp.int32, (ROWS, 128), 0)
    ids = jnp.zeros((ROWS, 128), jnp.int32)
    for r in range(ROWS):
        ids = jnp.where(sub == r, ids_ref[r // 2, 2 * z + r % 2], ids)
    id_send[...] = ids
    id_recv[0] = ids
    fsend[...] = jnp.zeros_like(fsend)

    for s in range(shots):
        loads[s].wait()
        for h in range(2):
            rows = pl.ds(s * per_shot + h * 128, 128)
            tr_hi[rows, :], tr_lo[rows, :] = split(tr[rows, :])
    for s in range(shots):
        wloads[s].wait()
    for r in range(ROWS):
        wt_hi[r], wt_lo[r] = split(wt[r])

    def make(s):
        odd = s % 2
        off = odd * ((7 - s) // 2) + (1 - odd) * (ZS - (8 - s) // 2)
        f = (z + off) % ZS
        turn = turn_ref[f]
        for q in range(4):
            cols = pl.ds(q * 256, 256)
            tc, ts = turn[0:1, q * 256 : q * 256 + 256], turn[1:2, q * 256 : q * 256 + 256]
            c0, s0 = base_ref[0:per, cols], base_ref[per:both, cols]
            hi, lo = split(c0 * tc - s0 * ts)
            table[0:per, cols] = hi
            table[both : both + per, cols] = lo
            hi, lo = split(-(s0 * tc + c0 * ts))
            table[per:both, cols] = hi
            table[both + per : 2 * both, cols] = lo
        for pair in range(4):
            rows = pl.ds(pair * 256, 256)
            big = nt_dot(table[...], tr_hi[rows, :])
            spec = big[0:both] + big[both:] + nt_dot(table[0:both, :], tr_lo[rows, :])
            for h in range(2):
                r = pair * 2 + h
                hi, lo = split(spec[:, h * 128 : h * 128 + 128])
                two = nn_dot(jnp.concatenate([hi, lo], axis=0), wt_hi[r])
                part = two[0:both] + two[both:] + nn_dot(hi, wt_lo[r])
                send[s, pl.ds(r, both, stride=ROWS), :] = part

    def block(p):
        return pl.ds(pl.multiple_of(p * share * ROWS, share * ROWS), share * ROWS)

    def post(s):
        pltpu.make_async_copy(send.at[s, block(me)], recv.at[s, 0], self_sem.at[s]).start()

        def one(r, carry):
            p = peer(r)
            pltpu.make_async_remote_copy(
                src_ref=send.at[s, block(p)],
                dst_ref=recv.at[s, r],
                send_sem=send_sem.at[s],
                recv_sem=recv_sem.at[s],
                device_id=(p, z),
                device_id_type=MESH,
            ).start()
            return carry

        lax.fori_loop(1, PLANE, one, 0)

    def take(s):
        pltpu.make_async_copy(send.at[s, block(me)], recv.at[s, 0], self_sem.at[s]).wait()
        got = recv.at[s, pl.ds(1, PLANE - 1)]
        pltpu.make_async_copy(got, got, recv_sem.at[s]).wait()
        for i in range(share):
            data = recv[s, :, i * ROWS : i * ROWS + ROWS, :].reshape(PLANE * ROWS, 128)
            hi, lo = split(data)
            sums = nn_dot(onehot[...], jnp.concatenate([hi, lo], axis=1))
            zsend[s, i * tiles : (i + 1) * tiles, :] = sums[:, 0:128] + sums[:, 128:256]

        @pl.when(s >= 2)
        def _():
            came = zrecv.at[s]
            pltpu.make_async_copy(came, came, zrecv_sem.at[s]).wait()
            zsend[s] = zsend[s] + zrecv[s]

        @pl.when(s < ZS - 1)
        def _():
            pltpu.make_async_remote_copy(
                src_ref=zsend.at[s],
                dst_ref=zrecv.at[s + 2],
                send_sem=zsend_sem.at[s],
                recv_sem=zrecv_sem.at[s + 2],
                device_id=(me, (z + ZS + 2 * (s % 2) - 1) % ZS),
                device_id_type=MESH,
            ).start()

    make(0)
    pl.semaphore_wait(barrier, PLANE - 1 + 2)

    def tell(r, carry):
        pltpu.make_async_remote_copy(
            src_ref=id_send,
            dst_ref=id_recv.at[r],
            send_sem=id_send_sem,
            recv_sem=id_recv_sem,
            device_id=(peer(r), z),
            device_id_type=MESH,
        ).start()
        return carry

    lax.fori_loop(1, PLANE, tell, 0)
    post(0)
    got_ids = id_recv.at[pl.ds(1, PLANE - 1)]

    def body(u, carry):
        @pl.when(u < ZS)
        def _():
            make(u)
            post(u)

        @pl.when(u == 1)
        def _():
            pltpu.make_async_copy(got_ids, got_ids, id_recv_sem).wait()
            lane = lax.broadcasted_iota(jnp.int32, (PLANE * ROWS, 128), 1)
            tile = jnp.where(lane < tiles, lane % PLANE * TILES_DEV + lane // PLANE, -1)
            hit = id_recv[...].reshape(PLANE * ROWS, 128) == tile
            turned = jnp.where(hit, 1.0, 0.0).astype(jnp.float32).T
            onehot[...] = turned[0:tiles].astype(jnp.bfloat16)

        @pl.when(u >= 2)
        def _():
            take(u - 2)

        return carry

    lax.fori_loop(1, ZS + 2, body, 0)

    last = zrecv.at[ZS]
    pltpu.make_async_copy(last, last, zrecv_sem.at[ZS]).wait()
    for i in range(share):
        rows = slice(i * tiles, (i + 1) * tiles)
        total = zsend[ZS - 1, rows, :] + zrecv[ZS, rows, :]
        for t in range(TILES_DEV):
            fsend[pl.ds(i * TILES_DEV + t, PLANE, stride=8), :] = total[
                t * PLANE : (t + 1) * PLANE
            ]

    def eight(p):
        return pl.ds(pl.multiple_of(p * 8, 8), 8)

    own = pltpu.make_async_copy(fsend.at[eight(me)], frecv.at[eight(me)], fself_sem)
    own.start()

    def finish(r, carry):
        p = peer(r)
        pltpu.make_async_remote_copy(
            src_ref=fsend.at[eight(p)],
            dst_ref=frecv.at[eight(me)],
            send_sem=fsend_sem,
            recv_sem=frecv_sem,
            device_id=(p, z),
            device_id_type=MESH,
        ).start()
        return carry

    lax.fori_loop(1, PLANE, finish, 0)
    own.wait()
    most = frecv.at[pl.ds(0, (PLANE - 1) * 8)]
    pltpu.make_async_copy(most, most, frecv_sem).wait()
    for t in range(TILES_DEV):
        for i in range(share):
            out_ref[t, pl.ds(i, PLANE, stride=share), :] = frecv[
                pl.ds(i * TILES_DEV + t, PLANE, stride=8), :
            ]

    pltpu.make_async_copy(most, most, fsend_sem).wait()
    pltpu.make_async_copy(got_ids, got_ids, id_send_sem).wait()

    def drain(s, carry):
        gone = send.at[s, pl.ds(0, (PLANE - 1) * share * ROWS)]
        pltpu.make_async_copy(gone, gone, send_sem.at[s]).wait()

        @pl.when(s < ZS - 1)
        def _():
            left = zsend.at[s]
            pltpu.make_async_copy(left, left, zsend_sem.at[s]).wait()

        return carry

    lax.fori_loop(0, ZS, drain, 0)


def shards(traces, interp_weights, tile_ids):
    shots, recs, time_len = traces.shape
    per = NF // ZS
    both = 2 * per
    share = both // PLANE
    tiles = PLANE * TILES_DEV
    block_len, tile_len = interp_weights.shape[2:]
    base, turn = tables(time_len, per)
    total = shots * recs
    vmem = pl.BlockSpec(memory_space=pltpu.VMEM)
    anywhere = pl.BlockSpec(memory_space=pl.ANY)
    dma = pltpu.SemaphoreType.DMA
    f32, bf16 = jnp.float32, jnp.bfloat16
    binned = pl.pallas_call(
        kernel,
        out_shape=jax.ShapeDtypeStruct((TILES_DEV, both, tile_len), f32),
        in_specs=[pl.BlockSpec(memory_space=pltpu.SMEM), vmem, vmem, anywhere, anywhere],
        out_specs=vmem,
        scratch_shapes=[
            pltpu.VMEM((total, time_len), f32),
            pltpu.VMEM((total, time_len), bf16),
            pltpu.VMEM((total, time_len), bf16),
            pltpu.VMEM((ROWS, block_len, tile_len), f32),
            pltpu.VMEM((ROWS, block_len, tile_len), bf16),
            pltpu.VMEM((ROWS, block_len, tile_len), bf16),
            pltpu.VMEM((2 * both, time_len), bf16),
            pltpu.VMEM((ZS, both * ROWS, tile_len), f32),
            pltpu.VMEM((ZS, PLANE, share * ROWS, tile_len), f32),
            pltpu.VMEM((ZS, share * tiles, tile_len), f32),
            pltpu.VMEM((ZS + 1, share * tiles, tile_len), f32),
            pltpu.VMEM((ROWS, 128), jnp.int32),
            pltpu.VMEM((PLANE, ROWS, 128), jnp.int32),
            pltpu.VMEM((tiles, PLANE * ROWS), bf16),
            pltpu.VMEM((PLANE * 8, tile_len), f32),
            pltpu.VMEM((PLANE * 8, tile_len), f32),
            dma((shots,)), dma((shots,)), dma((ZS,)), dma((ZS,)), dma((ZS,)),
            dma((ZS,)), dma((ZS + 1,)), dma, dma, dma, dma, dma,
        ],
        compiler_params=pltpu.CompilerParams(collective_id=0, has_side_effects=True),
    )(tile_ids, jnp.asarray(base), jnp.asarray(turn), traces, interp_weights)
    return binned.reshape(TILES_DEV, 2, per, tile_len)


def solution(mesh):
    in_specs = (P("shot", "freq", None), P("shot", None, None, None), P("shot", None))
    out_specs = P("shot", None, "freq", None)
    return jax.shard_map(shards, mesh=mesh, in_specs=in_specs, out_specs=out_specs, check_vma=False)
```

time: 243 us -> 59.4 us (0.24)
  waiting for transfers between devices: 145 us -> 0 us
  Pallas kernels: 0 us -> 57.3 us
  local copies, waits for them, and re-layouts: 36 us -> 1.54 us
  matrix products: 27.8 us -> 0 us
  starting transfers between devices: 24.1 us -> 0 us
  other arithmetic: 7.34 us -> 0 us
    all_to_all x3 -> x0, waiting for transfers between devices: 145 us -> none  [the longest x1 72.9 us: shards(): lax.all_to_all(spectrum, 'freq', split_axis=2, concat_axis=3, tiled=True)]
    pallas_call x0 -> x1, Pallas kernels: none -> 57.3 us  [shards(): pl.pallas_call(kernel, out_shape=jax.ShapeDtypeStruct((TILES_DEV, both, t...]
    dot_general x4 -> x0, matrix products: 27.8 us -> none  [the longest x1 12.1 us: shards(): spectrum = jnp.einsum('cft,srt->scfr', tables, traces, precision=highest)]
    all_to_all x3 -> x0, starting transfers between devices: 24.1 us -> none  [the longest x1 9.13 us: shards(): lax.all_to_all(spectrum, 'freq', split_axis=2, concat_axis=3, tiled=True)]
    dot_general x3 -> x0, local copies, waits for them, and re-layouts: 14 us -> none  [the longest x2 7.26 us: shards(): jnp.dot(landing, received.reshape(shot_count * cap_slots, width), precisi...]
    reshape x4 -> x0, local copies, waits for them, and re-layouts: 13.5 us -> none  [the longest x1 7.92 us: shards(): received.reshape(shot_count * cap_slots, width)]
    neg x1 -> x0, other arithmetic: 6.17 us -> none  [shards(): -jnp.sin(angle)]
    all_to_all x2 -> x0, local copies, waits for them, and re-layouts: 4 us -> none  [the longest x1 3.49 us: shards(): lax.all_to_all(spectrum, 'freq', split_axis=2, concat_axis=3, tiled=True)]
  transfers between devices with their start and end apart: 3 -> 0, of which waited for: 2 -> 0; matrix products, arithmetic and copies ran while one was open for 12% -> 0% of each run, Pallas kernels for 0% -> 0%
where the time goes in v1:
time: 59.4 us; the launch traced here: 58.9 us
  Pallas kernels  57.3 us (96%)
  local copies, waits for them, and re-layouts  1.54 us (3%)
    pallas_call x1, Pallas kernels, shards(): pl.pallas_call(kernel, out_shape=jax.ShapeDtypeStruct((TILES_DEV, both, t...  57.3 us
    unnamed x1, local copies, waits for them, and re-layouts  1.54 us

profile of v1, /device:TPU:1, one launch (start us, length us, event | category | flops | bytes accessed | tf_op | source)
XLA Modules:
  0.0 58.9 jit_solution(8713309493631268320)
XLA Ops:
  0.0 57.3 %shard_map.55 = f32[2,96,128]{2,1,0:T(8,128)} custom-call(s32[4,16]{1,0:T(4,128)} %ids_ref.1, f32[96,1024]{1,0:T(8,128)} %constant.4.clone.base_ref, f32[8,2,1024]{2,1,0:T(2,128)} %constant.5.clone.turn_ref, f32[4,256,1024]{2,1,0:T(8,128)} %traces_ref.1, f32[4,16,128,128]{3,2,1,0:T(8,128)} %weights_ref.1), custom_call_target="tpu_custom_call" | custom-call | tf_op jit(solution)/shard_map/pallas_call | solution.py:296
  57.3 1.5 %copy.7 = f32[2,2,48,128]{3,2,1,0:T(8,128)} copy(f32[2,2,48,128]{3,2,1,0:T(8,128)} %bitcast.1) | data formatting | bytes 196608

commit v2 on v1

v2 whole, which is shorter than its diff:
```python
import math

import jax
import jax.numpy as jnp
import numpy as np
from jax import lax
from jax.experimental import pallas as pl
from jax.experimental.pallas import tpu as pltpu
from jax.sharding import PartitionSpec as P

NF = 384
TILES_DEV = 2
YS, XS, CS = 4, 4, 2
PLANE = YS * XS * CS
ZS = 8
ROWS = 8
WIDE = 2
SIDE = 2
SLOT = 16
MESH = pl.DeviceIdType.MESH


def tables(time_len, per):
    t = np.arange(time_len)
    low = 2.0 * math.pi / time_len * (np.arange(per)[:, None] * t[None, :] % time_len)
    base = np.concatenate([np.cos(low), np.sin(low)]) / math.sqrt(time_len)
    high = 2.0 * math.pi / time_len * ((np.arange(ZS) * per)[:, None] * t[None, :] % time_len)
    turn = np.stack([np.cos(high), np.sin(high)], axis=1)
    return base.astype(np.float32), turn.astype(np.float32)


def split(value):
    high = value.astype(jnp.bfloat16)
    return high, (value - high.astype(jnp.float32)).astype(jnp.bfloat16)


def nt_dot(a, b):
    return lax.dot_general(a, b, (((1,), (1,)), ((), ())), preferred_element_type=jnp.float32)


def nn_dot(a, b):
    return jnp.dot(a, b, preferred_element_type=jnp.float32)


def kernel(
    ids_ref, base_hbm, turn_hbm, traces_ref, weights_ref, out_ref,
    base_ref, turn_ref, tr, tr_hi, tr_lo, wt, wt_hi, wt_lo, table, send, recv, xrecv, yrecv,
    zsend, zrecv, id_send, id_recv, onehot, yhot, fsend, frecv,
    table_sem, load_sem, wload_sem, send_sem, recv_sem, self_sem, xsend_sem, xrecv_sem, xself_sem,
    ysend_sem, yrecv_sem, yself_sem, zsend_sem, zrecv_sem,
    id_send_sem, id_recv_sem, fsend_sem, frecv_sem, fself_sem,
):
    per = base_ref.shape[0] // 2
    both = 2 * per
    parts = WIDE + 2 * SIDE
    xfrom = PLANE * WIDE
    yfrom = xfrom + XS * CS * SIDE
    tiles = PLANE * TILES_DEV
    me = lax.axis_index("shot")
    z = lax.axis_index("freq")
    core = me % CS
    x = me // CS % XS
    y = me // (CS * XS)

    rows_at = [(y + d) % YS * (XS * CS) for d in range(YS)]
    cols_at = [(x + d) % XS * CS for d in range(XS)]
    cores_at = [core, (core + 1) % CS]

    def peer(r):
        return rows_at[r // (CS * XS)] + cols_at[r // CS % XS] + cores_at[r % CS]

    far_first = sorted(
        range(1, PLANE),
        key=lambda r: -min(r // 8, 4 - r // 8) - min(r // 2 % 4, 4 - r // 2 % 4),
    )

    barrier = pltpu.get_barrier_semaphore()

    def greet(r):
        pl.semaphore_signal(barrier, inc=1, device_id=(peer(r), z), device_id_type=MESH)

    for r in far_first:
        greet(r)
    for step in (1, ZS - 1):
        pl.semaphore_signal(
            barrier, inc=1, device_id=(me, (z + step) % ZS), device_id_type=MESH
        )

    shots = traces_ref.shape[0]
    per_shot = traces_ref.shape[1]
    first = [
        pltpu.make_async_copy(base_hbm, base_ref, table_sem.at[0]),
        pltpu.make_async_copy(turn_hbm, turn_ref, table_sem.at[1]),
    ]
    for copy in first:
        copy.start()
    wloads = []
    for s in range(shots):
        wloads.append(
            pltpu.make_async_copy(
                weights_ref.at[s, pl.ds(2 * z, 2)], wt.at[pl.ds(2 * s, 2)], wload_sem.at[s]
            )
        )
        wloads[-1].start()

    loads = []
    for s in range(shots):
        loads.append(
            pltpu.make_async_copy(
                traces_ref.at[s], tr.at[pl.ds(s * per_shot, per_shot)], load_sem.at[s]
            )
        )
        loads[-1].start()
    lane = lax.broadcasted_iota(jnp.int32, (1, 128), 1)
    ids = jnp.zeros((1, 128), jnp.int32)
    for r in range(ROWS):
        ids = jnp.where(lane % ROWS == r, ids_ref[r // 2, 2 * z + r % 2], ids)
    id_send[...] = ids
    id_recv[0] = ids
    fsend[...] = jnp.zeros_like(fsend)

    def tabulate(s):
        odd = s % 2
        off = odd * ((7 - s) // 2) + (1 - odd) * (ZS - (8 - s) // 2)
        f = (z + off) % ZS
        turn = turn_ref[f]
        for q in range(4):
            cols = pl.ds(q * 256, 256)
            tc, ts = turn[0:1, q * 256 : q * 256 + 256], turn[1:2, q * 256 : q * 256 + 256]
            c0, s0 = base_ref[0:per, cols], base_ref[per:both, cols]
            hi, lo = split(c0 * tc - s0 * ts)
            table[0:per, cols] = hi
            table[both : both + per, cols] = lo
            hi, lo = split(-(s0 * tc + c0 * ts))
            table[per:both, cols] = hi
            table[both + per : 2 * both, cols] = lo

    def project(s, pair):
        rows = pl.ds(pair * 256, 256)
        big = nt_dot(table[...], tr_hi[rows, :])
        spec = big[0:both] + big[both:] + nt_dot(table[0:both, :], tr_lo[rows, :])
        for h in range(2):
            r = pair * 2 + h
            hi, lo = split(spec[:, h * 128 : h * 128 + 128])
            two = nn_dot(jnp.concatenate([hi, lo], axis=0), wt_hi[r])
            part = two[0:both] + two[both:] + nn_dot(hi, wt_lo[r])
            send[s, pl.ds(r, both, stride=ROWS), :] = part

    def make(s):
        tabulate(s)
        for pair in range(shots):
            project(s, pair)

    def make_first():
        for copy in first:
            copy.wait()
        tabulate(0)
        for s in range(shots):
            wloads[s].wait()
        for r in range(ROWS):
            wt_hi[r], wt_lo[r] = split(wt[r])
        for s in range(shots):
            loads[s].wait()
            for h in range(2):
                rows = pl.ds(s * per_shot + h * 128, 128)
                tr_hi[rows, :], tr_lo[rows, :] = split(tr[rows, :])
            project(0, s)

    def rows_of(first_row, index, count):
        start = pl.multiple_of((first_row + index * count) * ROWS, ROWS)
        return pl.ds(start, count * ROWS)

    def xpeer(j):
        index = cols_at[j // CS] + cores_at[j % CS]
        return index, rows_at[0] + index

    def ypeer(j):
        place, pc = rows_at[j // CS], cores_at[j % CS]
        return place // XS + pc, place + cols_at[0] + pc

    def own_copies(s):
        return [
            pltpu.make_async_copy(
                send.at[s, rows_of(0, me, WIDE)], recv.at[s, 0], self_sem.at[s]
            ),
            pltpu.make_async_copy(
                send.at[s, rows_of(xfrom, xpeer(0)[0], SIDE)], xrecv.at[s, 0], xself_sem.at[s]
            ),
            pltpu.make_async_copy(
                send.at[s, rows_of(yfrom, ypeer(0)[0], SIDE)], yrecv.at[s, 0], yself_sem.at[s]
            ),
        ]

    def post(s):
        for copy in own_copies(s):
            copy.start()

        def side(j):
            index, p = xpeer(j)
            pltpu.make_async_remote_copy(
                src_ref=send.at[s, rows_of(xfrom, index, SIDE)],
                dst_ref=xrecv.at[s, j],
                send_sem=xsend_sem.at[s],
                recv_sem=xrecv_sem.at[s],
                device_id=(p, z),
                device_id_type=MESH,
            ).start()
            index, p = ypeer(j)
            pltpu.make_async_remote_copy(
                src_ref=send.at[s, rows_of(yfrom, index, SIDE)],
                dst_ref=yrecv.at[s, j],
                send_sem=ysend_sem.at[s],
                recv_sem=yrecv_sem.at[s],
                device_id=(p, z),
                device_id_type=MESH,
            ).start()

        def one(r):
            p = peer(r)
            pltpu.make_async_remote_copy(
                src_ref=send.at[s, rows_of(0, p, WIDE)],
                dst_ref=recv.at[s, r],
                send_sem=send_sem.at[s],
                recv_sem=recv_sem.at[s],
                device_id=(p, z),
                device_id_type=MESH,
            ).start()

        for r in range(1, PLANE):
            one(r)
        for r in range(1, XS * CS):
            side(r)

    def gather(hot, data, s, part):
        hi, lo = split(data)
        sums = nn_dot(hot, jnp.concatenate([hi, lo], axis=1))
        zsend[s, part * tiles : (part + 1) * tiles, :] = sums[:, 0:128] + sums[:, 128:256]

    def take(s):
        for copy in own_copies(s):
            copy.wait()
        for ref, sem in ((xrecv, xrecv_sem), (yrecv, yrecv_sem), (recv, recv_sem)):
            got = ref.at[s, pl.ds(1, ref.shape[1] - 1)]
            pltpu.make_async_copy(got, got, sem.at[s]).wait()
        near = XS * CS * ROWS
        for i in range(SIDE):
            rows = slice(i * ROWS, i * ROWS + ROWS)
            gather(onehot[:, 0:near], xrecv[s, :, rows, :].reshape(near, 128), s, WIDE + i)
            gather(yhot[...], yrecv[s, :, rows, :].reshape(near, 128), s, WIDE + SIDE + i)
        for i in range(WIDE):
            data = recv[s, :, i * ROWS : i * ROWS + ROWS, :].reshape(PLANE * ROWS, 128)
            gather(onehot[...], data, s, i)

        @pl.when(s >= 2)
        def _():
            came = zrecv.at[s]
            pltpu.make_async_copy(came, came, zrecv_sem.at[s]).wait()
            zsend[s] = zsend[s] + zrecv[s]

        @pl.when(s < ZS - 1)
        def _():
            pltpu.make_async_remote_copy(
                src_ref=zsend.at[s],
                dst_ref=zrecv.at[s + 2],
                send_sem=zsend_sem.at[s],
                recv_sem=zrecv_sem.at[s + 2],
                device_id=(me, (z + ZS + 2 * (s % 2) - 1) % ZS),
                device_id_type=MESH,
            ).start()

    make_first()
    pl.semaphore_wait(barrier, PLANE - 1 + 2)

    def tell(r):
        pltpu.make_async_remote_copy(
            src_ref=id_send,
            dst_ref=id_recv.at[r],
            send_sem=id_send_sem,
            recv_sem=id_recv_sem,
            device_id=(peer(r), z),
            device_id_type=MESH,
        ).start()

    post(0)
    for r in far_first:
        tell(r)
    make(1)
    got_ids = id_recv.at[pl.ds(1, PLANE - 1)]

    def body(u, carry):
        @pl.when(u < ZS)
        def _():
            post(u)

        @pl.when(u < ZS - 1)
        def _():
            make(u + 1)

        @pl.when(u == 1)
        def _():
            pltpu.make_async_copy(got_ids, got_ids, id_recv_sem).wait()
            rho = lax.broadcasted_iota(jnp.int32, (tiles, 128), 0)
            tile = rho % PLANE * TILES_DEV + rho // PLANE
            for half in range(2):
                row = jnp.zeros((1, 128), jnp.int32)
                for slot in range(16):
                    row = jnp.where(lane // ROWS == slot, id_recv[half * 16 + slot], row)
                hit = jnp.where(tile == row, 1.0, 0.0).astype(jnp.float32)
                onehot[:, half * 128 : half * 128 + 128] = hit.astype(jnp.bfloat16)
            row = jnp.zeros((1, 128), jnp.int32)
            for j in range(YS * CS):
                row = jnp.where(lane // ROWS == j, id_recv[j // CS * XS * CS + j % CS], row)
            hit = jnp.where(tile == row, 1.0, 0.0).astype(jnp.float32)
            yhot[...] = hit[:, 0 : YS * CS * ROWS].astype(jnp.bfloat16)

        @pl.when(u >= 1)
        def _():
            take(u - 1)

        return carry

    lax.fori_loop(1, ZS + 1, body, 0)

    last = zrecv.at[ZS]
    pltpu.make_async_copy(last, last, zrecv_sem.at[ZS]).wait()
    for i in range(parts):
        rows = slice(i * tiles, (i + 1) * tiles)
        total = zsend[ZS - 1, rows, :] + zrecv[ZS, rows, :]
        for t in range(TILES_DEV):
            fsend[pl.ds(i * TILES_DEV + t, PLANE, stride=SLOT), :] = total[
                t * PLANE : (t + 1) * PLANE
            ]

    def slot(p):
        return pl.ds(pl.multiple_of(p * SLOT, SLOT), SLOT)

    own = pltpu.make_async_copy(fsend.at[slot(me)], frecv.at[slot(me)], fself_sem)
    own.start()

    def finish(r):
        p = peer(r)
        pltpu.make_async_remote_copy(
            src_ref=fsend.at[slot(p)],
            dst_ref=frecv.at[slot(me)],
            send_sem=fsend_sem,
            recv_sem=frecv_sem,
            device_id=(p, z),
            device_id_type=MESH,
        ).start()

    for r in far_first:
        finish(r)
    own.wait()
    most = frecv.at[pl.ds(0, (PLANE - 1) * SLOT)]
    pltpu.make_async_copy(most, most, frecv_sem).wait()
    for t in range(TILES_DEV):
        for i in range(WIDE):
            out_ref[t, pl.ds(i, PLANE, stride=WIDE), :] = frecv[
                pl.ds(i * TILES_DEV + t, PLANE, stride=SLOT), :
            ]
        for i in range(SIDE):
            row = (WIDE + i) * TILES_DEV + t
            count = XS * CS
            total = frecv[pl.ds(row, count, stride=SLOT), :]
            for py in range(1, YS):
                total = total + frecv[pl.ds(py * count * SLOT + row, count, stride=SLOT), :]
            out_ref[t, pl.ds(xfrom + i, count, stride=SIDE), :] = total
            row = (WIDE + SIDE + i) * TILES_DEV + t
            for pc in range(CS):
                total = frecv[pl.ds(pc * SLOT + row, YS, stride=count * SLOT), :]
                for px in range(1, XS):
                    start = (px * CS + pc) * SLOT + row
                    total = total + frecv[pl.ds(start, YS, stride=count * SLOT), :]
                out_ref[t, pl.ds(yfrom + pc * SIDE + i, YS, stride=CS * SIDE), :] = total

    pltpu.make_async_copy(most, most, fsend_sem).wait()
    pltpu.make_async_copy(got_ids, got_ids, id_send_sem).wait()

    def drain(s, carry):
        for ref, sem in ((xrecv, xsend_sem), (yrecv, ysend_sem), (recv, send_sem)):
            gone = ref.at[s, pl.ds(1, ref.shape[1] - 1)]
            pltpu.make_async_copy(gone, gone, sem.at[s]).wait()

        @pl.when(s < ZS - 1)
        def _():
            left = zsend.at[s]
            pltpu.make_async_copy(left, left, zsend_sem.at[s]).wait()

        return carry

    lax.fori_loop(0, ZS, drain, 0)


def shards(traces, interp_weights, tile_ids):
    shots, recs, time_len = traces.shape
    per = NF // ZS
    both = 2 * per
    parts = WIDE + 2 * SIDE
    tiles = PLANE * TILES_DEV
    block_len, tile_len = interp_weights.shape[2:]
    base, turn = tables(time_len, per)
    total = shots * recs
    vmem = pl.BlockSpec(memory_space=pltpu.VMEM)
    hbm = pl.BlockSpec(memory_space=pltpu.HBM)
    dma = pltpu.SemaphoreType.DMA
    f32, bf16 = jnp.float32, jnp.bfloat16
    binned = pl.pallas_call(
        kernel,
        out_shape=jax.ShapeDtypeStruct((TILES_DEV, both, tile_len), f32),
        in_specs=[pl.BlockSpec(memory_space=pltpu.SMEM)] + [hbm] * 4,
        out_specs=vmem,
        scratch_shapes=[
            pltpu.VMEM(base.shape, f32),
            pltpu.VMEM(turn.shape, f32),
            pltpu.VMEM((total, time_len), f32),
            pltpu.VMEM((total, time_len), bf16),
            pltpu.VMEM((total, time_len), bf16),
            pltpu.VMEM((ROWS, block_len, tile_len), f32),
            pltpu.VMEM((ROWS, block_len, tile_len), bf16),
            pltpu.VMEM((ROWS, block_len, tile_len), bf16),
            pltpu.VMEM((2 * both, time_len), bf16),
            pltpu.VMEM((ZS, both * ROWS, tile_len), f32),
            pltpu.VMEM((ZS, PLANE, WIDE * ROWS, tile_len), f32),
            pltpu.VMEM((ZS, XS * CS, SIDE * ROWS, tile_len), f32),
            pltpu.VMEM((ZS, YS * CS, SIDE * ROWS, tile_len), f32),
            pltpu.VMEM((ZS, parts * tiles, tile_len), f32),
            pltpu.VMEM((ZS + 1, parts * tiles, tile_len), f32),
            pltpu.VMEM((1, 128), jnp.int32),
            pltpu.VMEM((PLANE, 1, 128), jnp.int32),
            pltpu.VMEM((tiles, PLANE * ROWS), bf16),
            pltpu.VMEM((tiles, YS * CS * ROWS), bf16),
            pltpu.VMEM((PLANE * SLOT, tile_len), f32),
            pltpu.VMEM((PLANE * SLOT, tile_len), f32),
            dma((2,)), dma((shots,)), dma((shots,)), dma((ZS,)), dma((ZS,)), dma((ZS,)),
            dma((ZS,)), dma((ZS,)), dma((ZS,)), dma((ZS,)), dma((ZS,)), dma((ZS,)),
            dma((ZS,)), dma((ZS + 1,)), dma, dma, dma, dma, dma,
        ],
        compiler_params=pltpu.CompilerParams(collective_id=0, has_side_effects=True),
    )(tile_ids, jnp.asarray(base), jnp.asarray(turn), traces, interp_weights)
    return binned.reshape(TILES_DEV, 2, per, tile_len)


def solution(mesh):
    in_specs = (P("shot", "freq", None), P("shot", None, None, None), P("shot", None))
    out_specs = P("shot", None, "freq", None)
    return jax.shard_map(shards, mesh=mesh, in_specs=in_specs, out_specs=out_specs, check_vma=False)
```

time: 59.4 us -> 55.4 us (0.933)
  Pallas kernels: 57.3 us -> 53.7 us
    pallas_call x1, Pallas kernels: 57.3 us -> 53.7 us  [shards(): pl.pallas_call(kernel, out_shape=jax.ShapeDtypeStruct((TILES_DEV, both, t...]
where the time goes in v2:
time: 55.4 us; the launch traced here: 55.3 us
  Pallas kernels  53.7 us (97%)
  local copies, waits for them, and re-layouts  1.54 us (3%)
    pallas_call x1, Pallas kernels, shards(): pl.pallas_call(kernel, out_shape=jax.ShapeDtypeStruct((TILES_DEV, both, t...  53.7 us
    unnamed x1, local copies, waits for them, and re-layouts  1.54 us

profile of v2, /device:TPU:1, one launch (start us, length us, event | category | flops | bytes accessed | tf_op | source)
XLA Modules:
  0.0 55.3 jit_solution(3942831588058831544)
XLA Ops:
  0.0 53.7 %shard_map.55 = f32[2,96,128]{2,1,0:T(8,128)} custom-call(s32[4,16]{1,0:T(4,128)} %ids_ref.1, f32[96,1024]{1,0:T(8,128)} %constant.4.clone.base_hbm, f32[8,2,1024]{2,1,0:T(2,128)} %constant.5.clone.turn_hbm, f32[4,256,1024]{2,1,0:T(8,128)} %traces_ref.1, f32[4,16,128,128]{3,2,1,0:T(8,128)} %weights_ref.1), custom_call_target="tpu_custom_call" | custom-call | tf_op jit(solution)/shard_map/pallas_call | solution.py:407
  53.7 1.5 %copy.7 = f32[2,2,48,128]{3,2,1,0:T(8,128)} copy(f32[2,2,48,128]{3,2,1,0:T(8,128)} %bitcast.1) | data formatting | bytes 196608

commit v3 on v2

--- a/solution.py
+++ b/solution.py
@@ -282,9 +282,9 @@
         ).start()
 
     post(0)
+    make(1)
     for r in far_first:
         tell(r)
-    make(1)
     got_ids = id_recv.at[pl.ds(1, PLANE - 1)]
 
     def body(u, carry):
@@ -332,7 +332,7 @@
             ]
 
     def slot(p):
-        return pl.ds(pl.multiple_of(p * SLOT, SLOT), SLOT)
+        return pl.ds(pl.multiple_of(p * SLOT, SLOT), parts * TILES_DEV)
 
     own = pltpu.make_async_copy(fsend.at[slot(me)], frecv.at[slot(me)], fself_sem)
     own.start()
@@ -350,8 +350,24 @@
 
     for r in far_first:
         finish(r)
+    pltpu.make_async_copy(got_ids, got_ids, id_send_sem).wait()
+
+    def drain(s, carry):
+        for ref, sem in ((xrecv, xsend_sem), (yrecv, ysend_sem), (recv, send_sem)):
+            gone = ref.at[s, pl.ds(1, ref.shape[1] - 1)]
+            pltpu.make_async_copy(gone, gone, sem.at[s]).wait()
+
+        @pl.when(s < ZS - 1)
+        def _():
+            left = zsend.at[s]
+            pltpu.make_async_copy(left, left, zsend_sem.at[s]).wait()
+
+        return carry
+
+    lax.fori_loop(0, ZS, drain, 0)
+
     own.wait()
-    most = frecv.at[pl.ds(0, (PLANE - 1) * SLOT)]
+    most = frecv.at[pl.ds(0, (PLANE - 1) * parts * TILES_DEV)]
     pltpu.make_async_copy(most, most, frecv_sem).wait()
     for t in range(TILES_DEV):
         for i in range(WIDE):
@@ -374,21 +390,6 @@
                 out_ref[t, pl.ds(yfrom + pc * SIDE + i, YS, stride=CS * SIDE), :] = total
 
     pltpu.make_async_copy(most, most, fsend_sem).wait()
-    pltpu.make_async_copy(got_ids, got_ids, id_send_sem).wait()
-
-    def drain(s, carry):
-        for ref, sem in ((xrecv, xsend_sem), (yrecv, ysend_sem), (recv, send_sem)):
-            gone = ref.at[s, pl.ds(1, ref.shape[1] - 1)]
-            pltpu.make_async_copy(gone, gone, sem.at[s]).wait()
-
-        @pl.when(s < ZS - 1)
-        def _():
-            left = zsend.at[s]
-            pltpu.make_async_copy(left, left, zsend_sem.at[s]).wait()
-
-        return carry
-
-    lax.fori_loop(0, ZS, drain, 0)
 
 
 def shards(traces, interp_weights, tile_ids):

time: 55.4 us -> 55.6 us (level)
  no operation moved by 1% of the time
where the time goes in v3:
time: 55.6 us; the launch traced here: 55.5 us
  Pallas kernels  54 us (97%)
  local copies, waits for them, and re-layouts  1.54 us (3%)
    pallas_call x1, Pallas kernels, shards(): pl.pallas_call(kernel, out_shape=jax.ShapeDtypeStruct((TILES_DEV, both, t...  54 us
    unnamed x1, local copies, waits for them, and re-layouts  1.54 us

profile of v3, /device:TPU:1, one launch (start us, length us, event | category | flops | bytes accessed | tf_op | source)
XLA Modules:
  0.0 55.5 jit_solution(3693463622933604977)
XLA Ops:
  0.0 54.0 %shard_map.55 = f32[2,96,128]{2,1,0:T(8,128)} custom-call(s32[4,16]{1,0:T(4,128)} %ids_ref.1, f32[96,1024]{1,0:T(8,128)} %constant.4.clone.base_hbm, f32[8,2,1024]{2,1,0:T(2,128)} %constant.5.clone.turn_hbm, f32[4,256,1024]{2,1,0:T(8,128)} %traces_ref.1, f32[4,16,128,128]{3,2,1,0:T(8,128)} %weights_ref.1), custom_call_target="tpu_custom_call" | custom-call | tf_op jit(solution)/shard_map/pallas_call | solution.py:408
  54.0 1.5 %copy.7 = f32[2,2,48,128]{3,2,1,0:T(8,128)} copy(f32[2,2,48,128]{3,2,1,0:T(8,128)} %bitcast.1) | data formatting | bytes 196608
